TPU v7x, 256 devices: a whole 4x4x8 slice. The times are simulated.
256 devices in a mesh: group: 32 (over x, y, core), mp: 8 (over z).
Axes of the slice: x: 4, y: 4, z: 8, core: 2. Of those that a mesh axis runs over, the one named last changes fastest.
Arguments:
- hidden: bfloat16 [16384, 1792], P('group')
- norm_gain: float32 [1792], replicated, may hold values from 0.1 to 1.9
- qkv_weight: bfloat16 [1792, 2304], P(None, 'mp'), may hold values from -0.125 to 0.125
- out_weight: bfloat16 [1792, 1792], P('mp'), may hold values from -0.125 to 0.125
- adapter_down: bfloat16 [1792, 1024], P(None, 'mp'), may hold values from -0.125 to 0.125
- adapter_up: bfloat16 [1024, 1792], P('mp'), may hold values from -1.5 to 1.5
- vocab_rows: bfloat16 [4096, 1792], P(('group', 'mp')), may hold values from -0.125 to 0.125
- segments: int32 [16384], P('group'), may hold values from 0 to 127, never falling along the last dimension, each value on 1 to 512 neighbouring positions
- request_adapter: int32 [128], replicated, may hold values from 0 to 63
- adapter_slot: int32 [64], replicated, may hold values from 0 to 63, each once
- page_table: int32 [2048], replicated, may hold values from 0 to 2047, as said below
Outputs:
- layer_update: bfloat16 [16384, 1792], P('group', 'mp')
- state_norms: float32 [16, 16384], P('mp', 'group')
- max_logits: float32 [16384], P(('group', 'mp'))
Inputs may be any that keep to these rules, and one draw needn't show every extreme that they name: A permutation of all pages. Logical page k of group g (entry g * 64 + k) lies in group page_table[g * 64 + k] // 64, and every group holds exactly two of the logical pages of every group. `segments`: every request's tokens stand together and in order; no request has more than 512 tokens. `adapter_slot`: A permutation.
All inputs are finite; a program needn't handle non-finite values.
Results may differ from a plain program's by a relative error of at most 0.013.
Values may be sent and summed in bfloat16 or wider, within the bound.
A program may use at most 64 MiB of HBM per device.

v0:
```python
import jax
import jax.numpy as jnp
from jax import lax
from jax.sharding import PartitionSpec as P

FEAT = 16
HD = 112
RANK = 16
EPSILON = 1e-05
PRECISE = lax.Precision.HIGHEST


def from_behind(value, axis, by):
    size = lax.axis_size(axis)
    pairs = [(i, i + by) for i in range(size) if 0 <= i + by < size]
    return lax.ppermute(value, axis, pairs)


def rms_normed(values, norm_gain):
    wide = values.astype(jnp.float32)
    meansq = jnp.mean(wide * wide, axis=-1, keepdims=True)
    return (wide * lax.rsqrt(meansq + EPSILON) * norm_gain).astype(jnp.bfloat16)


def features(vectors, feat_width):
    linear_part = vectors / feat_width**0.25
    outer_part = (vectors[..., :, None] * vectors[..., None, :]).reshape(
        vectors.shape[:-1] + (feat_width * feat_width,)
    )
    outer_part = outer_part / (2.0 * feat_width) ** 0.5
    ones_part = jnp.ones(vectors.shape[:-1] + (1,), jnp.float32)
    return jnp.concatenate([ones_part, linear_part, outer_part], axis=-1)


def block_step(state_carry, block_inputs, feat_width):
    states, totals, owner_seg = state_carry
    phi_query, phi_key, query_rows, key_rows, value_rows, seg_ids = block_inputs
    scaling = feat_width ** (-0.5)
    block_len = seg_ids.shape[0]
    position = jnp.arange(block_len, dtype=jnp.int32)
    allowed = (
        (position[:, None] >= position[None, :]) & (seg_ids[:, None] == seg_ids[None, :])
    ).astype(jnp.float32)
    carried = (seg_ids == owner_seg).astype(jnp.float32)[None, :]
    scores = jnp.einsum("hcf,hdf->hcd", query_rows, key_rows, precision=PRECISE) * scaling
    weights = (1.0 + scores + 0.5 * scores * scores) * allowed[None]
    numerator = jnp.einsum("hcd,hde->hce", weights, value_rows, precision=PRECISE)
    numerator = numerator + carried[..., None] * jnp.einsum(
        "hcp,hpe->hce", phi_query, states, precision=PRECISE
    )
    denominator = jnp.sum(weights, axis=-1) + carried * jnp.einsum(
        "hcp,hp->hc", phi_query, totals, precision=PRECISE
    )
    mixed_out = numerator / denominator[..., None]
    key_scores = jnp.einsum("hcf,hdf->hcd", key_rows, key_rows, precision=PRECISE) * scaling
    value_gram = jnp.einsum("hce,hde->hcd", value_rows, value_rows, precision=PRECISE)
    key_gram = (1.0 + key_scores + 0.5 * key_scores * key_scores) * value_gram
    masked_gram = jnp.einsum("cd,hde->hce", allowed, key_gram, precision=PRECISE)
    local_squares = jnp.sum(masked_gram * allowed[None], axis=-1)
    along = jnp.sum(
        jnp.einsum("hcp,hpe->hce", phi_key, states, precision=PRECISE) * value_rows, axis=-1
    )
    cross_squares = jnp.einsum("cd,hd->hc", allowed, along, precision=PRECISE)
    state_squares = jnp.sum(states * states, axis=(1, 2))
    squares = carried * (state_squares[:, None] + 2.0 * cross_squares) + local_squares
    counted = carried * totals[:, :1] + jnp.sum(allowed, axis=-1)[None, :]
    state_norm = jnp.sqrt(squares / (counted * (feat_width * value_rows.shape[-1])))
    last_seg = seg_ids[-1]
    member = (seg_ids == last_seg).astype(jnp.float32)
    continues = (owner_seg == last_seg).astype(jnp.float32)
    new_states = continues * states + jnp.einsum(
        "hcp,hce->hpe", phi_key * member[None, :, None], value_rows, precision=PRECISE
    )
    new_totals = continues * totals + jnp.einsum("hcp,c->hp", phi_key, member, precision=PRECISE)
    return ((new_states, new_totals, last_seg), (mixed_out, state_norm))


def best_of(candidates, piece):
    logits = jnp.einsum("rd,vd->rv", candidates, piece, preferred_element_type=jnp.float32)
    return jnp.max(logits, axis=1)


def on_device(
    hidden,
    norm_gain,
    qkv_weight,
    out_weight,
    adapter_down,
    adapter_up,
    vocab_rows,
    segments,
    request_adapter,
    adapter_slot,
    page_table,
):
    groups = lax.axis_size("group")
    own_group = lax.axis_index("group")
    shards = lax.axis_size("mp")
    own_shard = lax.axis_index("mp")
    rows_here = segments.shape[0]
    model_width = hidden.shape[1]
    slice_width = model_width // shards
    table = page_table.reshape(groups, -1)
    per_group = table.shape[1]
    per_peer = per_group // groups
    page_len = rows_here // per_group
    holders = table // per_group
    position = jnp.arange(per_group, dtype=jnp.int32)
    sort_keys = jnp.where(holders == own_group, position[None, :], per_group + position[None, :])
    ranked = jnp.argsort(sort_keys, axis=1)[:, :per_peer]
    picked = jnp.take_along_axis(table, ranked, axis=1) - own_group * per_group
    outgoing = hidden.reshape(per_group, page_len, model_width)[picked]
    normed_pages = rms_normed(outgoing, norm_gain)
    projected_pages = jnp.einsum(
        "abrd,dc->abrc", normed_pages, qkv_weight, preferred_element_type=jnp.float32
    ).astype(jnp.bfloat16)
    lowered_pages = jnp.einsum(
        "abrd,dc->abrc", normed_pages, adapter_down, preferred_element_type=jnp.float32
    ).astype(jnp.bfloat16)
    kept_pages = lax.dynamic_slice_in_dim(outgoing, own_shard * slice_width, slice_width, 3)
    widths = (kept_pages.shape[3], projected_pages.shape[3], lowered_pages.shape[3])
    packed = lax.all_to_all(
        jnp.concatenate([kept_pages, projected_pages, lowered_pages], axis=3),
        "group",
        split_axis=0,
        concat_axis=0,
        tiled=True,
    )
    arrived = (
        packed[..., : widths[0]],
        packed[..., widths[0] : widths[0] + widths[1]],
        packed[..., widths[0] + widths[1] :],
    )
    own_holders = lax.dynamic_index_in_dim(holders, own_group, 0, keepdims=False)
    onehot = (own_holders[:, None] == jnp.arange(groups, dtype=jnp.int32)[None, :]).astype(
        jnp.int32
    )
    earlier = jnp.sum((jnp.cumsum(onehot, axis=0) - onehot) * onehot, axis=1)
    source_rows = own_holders * per_peer + earlier

    def placed(received):
        gathered_rows = received.reshape((groups * per_peer,) + received.shape[2:])[source_rows]
        return gathered_rows.reshape((rows_here,) + received.shape[3:])

    residual, projected, lowered = [placed(received) for received in arrived]
    group_vocab = lax.all_gather(vocab_rows, "group", axis=0, tiled=True)
    heads_here = projected.shape[1] // (2 * FEAT + HD)
    split_heads = jnp.transpose(
        projected.reshape(rows_here, heads_here, 2 * FEAT + HD).astype(jnp.float32), (1, 0, 2)
    )
    query_rows = split_heads[..., :FEAT]
    key_rows = split_heads[..., FEAT : 2 * FEAT]
    value_rows = split_heads[..., 2 * FEAT :]
    phi_query = features(query_rows, FEAT)
    phi_key = features(key_rows, FEAT)
    last_seg = segments[-1]
    member = (segments == last_seg).astype(jnp.float32)
    end_state = jnp.einsum(
        "hcp,hce->hpe", phi_key * member[None, :, None], value_rows, precision=PRECISE
    )
    end_totals = jnp.einsum("hcp,c->hp", phi_key, member, precision=PRECISE)
    end_tag = jnp.reshape(last_seg + 1, (1,)).astype(jnp.float32)
    state_size, totals_size = (end_state.size, end_totals.size)
    handed = from_behind(
        jnp.concatenate([end_state.reshape(-1), end_totals.reshape(-1), end_tag]).astype(
            jnp.bfloat16
        ),
        "group",
        1,
    ).astype(jnp.float32)
    got_state = handed[:state_size].reshape(end_state.shape)
    got_totals = handed[state_size : state_size + totals_size].reshape(end_totals.shape)
    got_tag = handed[state_size + totals_size :]
    initial = (got_state, got_totals, got_tag[0].astype(jnp.int32) - 1)
    block_len = min(256, rows_here)
    blocks = rows_here // block_len

    def regroup(values):
        return jnp.transpose(
            values.reshape(values.shape[0], blocks, block_len, values.shape[-1]), (1, 0, 2, 3)
        )

    scan_inputs = (
        regroup(phi_query),
        regroup(phi_key),
        regroup(query_rows),
        regroup(key_rows),
        regroup(value_rows),
        segments.reshape(blocks, block_len),
    )

    def scan_step(state_carry, block_inputs):
        return block_step(state_carry, block_inputs, FEAT)

    _, (mixed_out, state_norm) = lax.scan(scan_step, initial, scan_inputs)
    attended = (
        jnp.transpose(mixed_out, (0, 2, 1, 3))
        .reshape(rows_here, heads_here * HD)
        .astype(jnp.bfloat16)
    )
    group_vocab, attended = lax.optimization_barrier((group_vocab, attended))
    state_norms = jnp.transpose(state_norm, (1, 0, 2)).reshape(heads_here, rows_here)
    request_ids = jnp.arange(request_adapter.shape[0], dtype=jnp.int32)
    adapter_of = jnp.sum(
        jnp.where(segments[:, None] == request_ids[None, :], request_adapter[None, :], 0), axis=1
    )
    adapter_ids = jnp.arange(adapter_slot.shape[0], dtype=jnp.int32)
    slot_ids = jnp.sum(
        jnp.where(adapter_of[:, None] == adapter_ids[None, :], adapter_slot[None, :], 0), axis=1
    )
    column_slot = jnp.arange(lowered.shape[1], dtype=jnp.int32) // RANK
    local_slot = slot_ids - own_shard * (lowered.shape[1] // RANK)
    low_rank = jnp.where(
        local_slot[:, None] == column_slot[None, :], lowered, jnp.zeros_like(lowered)
    )
    partial_value = jnp.dot(attended, out_weight, preferred_element_type=jnp.float32)
    partial_value = partial_value + jnp.dot(
        low_rank, adapter_up, preferred_element_type=jnp.float32
    )
    summed = lax.psum_scatter(
        partial_value.astype(jnp.bfloat16), "mp", scatter_dimension=1, tiled=True
    )
    final_rows = (residual.astype(jnp.float32) + summed.astype(jnp.float32)).astype(jnp.bfloat16)
    group_rows = lax.all_gather(final_rows, "mp", axis=1, tiled=True)
    partial_best = best_of(group_rows, group_vocab)
    max_logits = lax.dynamic_slice_in_dim(
        lax.pmax(partial_best, "mp"), own_shard * (rows_here // shards), rows_here // shards
    )
    return (summed, state_norms, max_logits)


def solution(mesh):
    placed = (
        P("group", None),
        P(),
        P(None, "mp"),
        P("mp", None),
        P(None, "mp"),
        P("mp", None),
        P(("group", "mp"), None),
        P("group"),
        P(),
        P(),
        P(),
    )
    return jax.shard_map(
        on_device,
        mesh=mesh,
        in_specs=placed,
        out_specs=(P("group", "mp"), P("mp", "group"), P(("group", "mp"))),
        check_vma=False,
    )
```

profile of v0, /device:TPU:2, one launch (start us, length us, event | category | flops | bytes accessed | tf_op | source)
XLA Modules:
  0.0 208.3 jit_solution(18308353681001285271)
XLA Ops:
  11.3 1.9 gather_fusion
  13.2 2.0 fusion.49
  16.6 2.3 %fusion.59 = bf16[32,2,8,128]{3,2,1,0:T(8,128)(2,1)S(1)} fusion(bf16[32,2,8,1792]{3,2,1,0:T(8,128)(2,1)} %bitcast.225, f32[1792]{0:T(1024)S(1)} %copy-done.16, f32[32,2,8]{2,1,0:T(2,128)S(1)} %copy.93, bf16[1792,128]{1,0:T(8,128)(2,1)S(1)} %copy-done.15), kind=kOutput, calls=%fused_computation.84 | convolution fusion | flops 238616576 | bytes 2434048 | tf_op jit(solution)/shard_map/abrd,dc->abrc/dot_general | solution.py:117
  21.3 7.6 %all-to-all-start = ((bf16[32,2,8,640]{3,2,1,0:T(8,128)(2,1)}), bf16[32,2,8,640]{3,2,1,0:T(8,128)(2,1)S(1)}, u32[]{:S(2)}, u32[]{:S(2)}) async-start(bf16[32,2,8,640]{3,2,1,0:T(8,128)(2,1)} %pad_maximum_fusion.2), calls=%async_computation | async-start | bytes 1310720 | tf_op jit(solution)/shard_map/all_to_all | solution.py:122
  31.7 8.4 %all-to-all-done = bf16[32,2,8,640]{3,2,1,0:T(8,128)(2,1)S(1)} async-done(((bf16[32,2,8,640]{3,2,1,0:T(8,128)(2,1)}), bf16[32,2,8,640]{3,2,1,0:T(8,128)(2,1)S(1)}, u32[]{:S(2)}, u32[]{:S(2)}) %all-to-all-start) | async-done | bytes 655392 | tf_op jit(solution)/shard_map/all_to_all | solution.py:122
  40.3 1.4 gather_fusion.1
  41.7 1.2 reshape_reshape.3
  44.1 1.3 gather_fusion.2
  45.7 2.2 %pad_maximum_fusion.1 = (f32[2,512,273]{1,2,0:T(8,128)}, f32[2,512,273]{1,2,0:T(8,128)S(1)}) fusion(f32[2,512,256]{1,2,0:T(8,128)S(1)} %bitcast.227, f32[2,512,16]{1,2,0:T(8,128)} %get-tuple-element.273, f32[273]{0:T(512)S(1)} %pad.3.clone, f32[2,512,256]{1,2,0:T(8,128)S(1)} %bitcast.228, f32[2,512,16]{1,2,0:T(8,128)} %get-tuple-element.274), kind=kLoop, calls=%fused_computation.86 | loop fusion | flops 1118208 | bytes 4465732 | tf_op jit(solution)/shard_map/concatenate | solution.py:32
  47.9 1.7 reshape.256
  49.6 2.3 %convolution_convert_fusion = bf16[2,273,112]{2,1,0:T(8,128)(2,1)} fusion(f32[2,512,273]{1,2,0:T(8,128)S(1)} %get-tuple-element.280, f32[512]{0:T(512)S(1)} %get-tuple-element.265, bf16[2,512,144]{1,2,0:T(8,128)(2,1)} %bitcast.230), kind=kOutput, calls=%fused_computation.83 | convolution fusion | flops 376058592 | bytes 1471936 | tf_op jit(solution)/shard_map/hcp,hce->hpe/dot_general | solution.py:158
  51.9 1.8 reshape.251
  53.7 3.0 %reshape.260 = f32[2,2,256,273]{2,1,3,0:T(2,128)} reshape(f32[2,512,273]{1,2,0:T(8,128)} %get-tuple-element.279) | data formatting | bytes 2236416 | tf_op jit(solution)/shard_map/reshape | solution.py:180
  57.4 2.1 concatenate.15
  59.5 2.9 %collective-permute-start = (bf16[61699]{0:T(1024)(128)(2,1)S(1)}, bf16[61699]{0:T(1024)(128)(2,1)S(1)}, u32[]{:S(2)}, u32[]{:S(2)}) collective-permute-start(bf16[61699]{0:T(1024)(128)(2,1)S(1)} %concatenate.15), channel_id=1, source_target_pairs={{0,8},{8,16},{16,24},{24,32},{32,40},{40,48},{48,56},{56,64},{64,7... | collective-permute-start | bytes 370202 | tf_op jit(solution)/shard_map/ppermute | solution.py:16
  63.3 4.5 %collective-permute-done = bf16[61699]{0:T(1024)(128)(2,1)S(1)} collective-permute-done((bf16[61699]{0:T(1024)(128)(2,1)S(1)}, bf16[61699]{0:T(1024)(128)(2,1)S(1)}, u32[]{:S(2)}, u32[]{:S(2)}) %collective-permute-start) | collective-permute-done | bytes 123430 | tf_op jit(solution)/shard_map/ppermute | solution.py:16
  69.6 24.2 %while.21 = (s32[]{:T(128)}, f32[2,273,112]{2,1,0:T(8,128)S(1)}, f32[2,273]{0,1:T(8,128)S(1)}, s32[]{:T(128)}, bf16[2,2,256,112]{2,3,1,0:T(8,128)(2,1)}, /*index...) while((s32[]{:T(128)}, f32[2,273,112]{2,1,0:T(8,128)S(1)}, ...), condition=%wide.region_10.11_spmd, body=%wide.region_4.10_spmd.sunk | while | flops 1377437056 | bytes 23302216 | solution.py:195
  95.1 1.9 fusion.81
  97.1 2.0 add_convert_fusion
  100.8 40.0 %reduce-scatter.2.cloned.1.call-done = bf16[512,224]{0,1:T(8,128)(2,1)} async-done(((bf16[512,1792]{0,1:T(8,128)(2,1)}), bf16[512,224]{0,1:T(8,128)(2,1)}) %reduce-scatter.2.cloned.1.call-update) | async-done | bytes 229392 | tf_op jit(solution)/shard_map/reduce_scatter | solution.py:220
  140.9 1.7 add_convert_fusion.1
  142.6 39.3 %all-gather.5.cloned.1.call-done = bf16[512,1792]{0,1:T(8,128)(2,1)} async-done(((bf16[512,224]{0,1:T(8,128)(2,1)}), bf16[512,1792]{0,1:T(8,128)(2,1)}) %all-gather.5.cloned.1.call-update) | async-done | bytes 1835024 | tf_op jit(solution)/shard_map/all_gather | solution.py:224
  181.9 3.2 %convolution_reduce_fusion = f32[512]{0:T(512)S(1)} fusion(bf16[512,1792]{1,0:T(8,128)(2,1)} %all-gather.3.cloned.1.call-done, bf16[512,1792]{0,1:T(8,128)(2,1)} %all-gather.5.cloned.1.call-done), kind=kOutput, calls=%fused_computation.82 | convolution fusion | flops 939785728 | bytes 3672064 | tf_op jit(solution)/shard_map/rd,vd->rv/dot_general | solution.py:79
  185.1 16.1 %pmax.7 = f32[512]{0:T(512)S(1)} all-reduce(f32[512]{0:T(512)S(1)} %convolution_reduce_fusion), channel_id=1, replica_groups=mesh['group'=32,'mp'=8] {'mp'}, use_global_device_ids=true, to_apply=%region_15.16 | all-reduce | flops 512 | bytes 4096 | tf_op jit(solution)/shard_map/pmax | solution.py:227
  (164 shorter events, 39.0 us)
Async XLA Ops:
  7.2 4.1 %copy-start = (bf16[512,1792]{1,0:T(8,128)(2,1)S(1)}, bf16[512,1792]{1,0:T(8,128)(2,1)}, u32[]{:S(2)}) copy-start(bf16[512,1792]{1,0:T(8,128)(2,1)} %param.13) | copy-start | bytes 5505028
  7.2 87.9 %all-gather.3.cloned.1.call-start = ((), (), s32[]{:S(2)}) async-start(), calls=%async_computation.2 | async-start | bytes 1892352 | tf_op jit(solution)/shard_map/all_gather | solution.py:146
  13.2 3.3 %copy-start.15 = (bf16[1792,128]{1,0:T(8,128)(2,1)S(1)}, bf16[1792,128]{1,0:T(8,128)(2,1)}, u32[]{:S(2)}) copy-start(bf16[1792,128]{1,0:T(8,128)(2,1)} %param.17) | copy-start | bytes 1376260
  13.2 3.3 %copy-start.16 = (f32[1792]{0:T(1024)S(1)}, f32[1792]{0:T(1024)}, u32[]{:S(2)}) copy-start(f32[1792]{0:T(1024)} %param.14) | copy-start | bytes 21508
  16.5 2.4 %copy-start.3 = (bf16[64,8,1792]{2,1,0:T(8,128)(2,1)S(1)}, bf16[64,8,1792]{2,1,0:T(8,128)(2,1)}, u32[]{:S(2)}) copy-start(bf16[64,8,1792]{2,1,0:T(8,128)(2,1)} %gather_fusion) | copy-start | bytes 5505028
  16.6 2.4 %copy-start.14 = (bf16[1792,288]{0,1:T(8,128)(2,1)S(1)}, bf16[1792,288]{0,1:T(8,128)(2,1)}, u32[]{:S(2)}) copy-start(bf16[1792,288]{0,1:T(8,128)(2,1)} %param.15) | copy-start | bytes 3096580
  20.1 8.9 %copy-start.11 = (s32[512]{0:T(512)S(1)}, s32[512]{0:T(512)}, u32[]{:S(2)}) copy-start(s32[512]{0:T(512)} %param.20) | copy-start | bytes 6148
  20.1 11.2 %copy-start.12 = (s32[128]{0:T(128)S(1)}, s32[128]{0:T(128)}, u32[]{:S(2)}) copy-start(s32[128]{0:T(128)} %param.21) | copy-start | bytes 1540
  20.1 11.4 %copy-start.13 = (s32[64]{0:T(128)S(1)}, s32[64]{0:T(128)}, u32[]{:S(2)}) copy-start(s32[64]{0:T(128)} %param.22) | copy-start | bytes 772
  21.3 18.8 %all-to-all-start = ((bf16[32,2,8,640]{3,2,1,0:T(8,128)(2,1)}), bf16[32,2,8,640]{3,2,1,0:T(8,128)(2,1)S(1)}, u32[]{:S(2)}, u32[]{:S(2)}) async-start(bf16[32,2,8,640]{3,2,1,0:T(8,128)(2,1)} %pad_maximum_fusion.2), calls=%async_computation | async-start | bytes 1310720 | tf_op jit(solution)/shard_map/all_to_all | solution.py:122
  28.9 112.0 %reduce-scatter.2.cloned.1.call-start = ((), (), s32[]{:S(2)}) async-start(), calls=%async_computation.3 | async-start | bytes 2064384 | tf_op jit(solution)/shard_map/reduce_scatter | solution.py:220
  40.1 4.0 %copy-start.4 = (bf16[32,2,8,640]{3,2,1,0:T(8,128)(2,1)}, bf16[32,2,8,640]{3,2,1,0:T(8,128)(2,1)S(1)}, u32[]{:S(2)}) copy-start(bf16[32,2,8,640]{3,2,1,0:T(8,128)(2,1)S(1)} %all-to-all-done) | copy-start | bytes 1966084
  43.3 2.4 %copy-start.5 = (bf16[512,2,144]{0,2,1:T(8,128)(2,1)}, bf16[512,2,144]{0,2,1:T(8,128)(2,1)S(1)}, u32[]{:S(2)}) copy-start(bf16[512,2,144]{0,2,1:T(8,128)(2,1)S(1)} %copy.94) | copy-start | bytes 884740
  59.5 8.3 %collective-permute-start = (bf16[61699]{0:T(1024)(128)(2,1)S(1)}, bf16[61699]{0:T(1024)(128)(2,1)S(1)}, u32[]{:S(2)}, u32[]{:S(2)}) collective-permute-start(bf16[61699]{0:T(1024)(128)(2,1)S(1)} %concatenate.15), channel_id=1, source_target_pairs={{0,8},{8,16},{16,24},{24,32},{32,40},{40,48},{48,56},{56,64},{64,7... | collective-permute-start | bytes 370202 | tf_op jit(solution)/shard_map/ppermute | solution.py:16
  72.3 2.6 %copy-start.1 = (f32[2,2,256,273]{2,0,3,1:T(2,128)S(1)}, f32[2,2,256,273]{2,0,3,1:T(2,128)}, u32[]{:S(2)}) copy-start(f32[2,2,256,273]{2,0,3,1:T(2,128)} %get-tuple-element.411) | copy-start | bytes 3354628 | tf_op jit(solution)/shard_map/while
  72.3 2.6 %copy-start.2 = (f32[2,2,256,273]{2,0,3,1:T(2,128)S(1)}, f32[2,2,256,273]{2,0,3,1:T(2,128)}, u32[]{:S(2)}) copy-start(f32[2,2,256,273]{2,0,3,1:T(2,128)} %get-tuple-element.415) | copy-start | bytes 3354628 | tf_op jit(solution)/shard_map/while
  74.8 2.5 %copy-start.9 = (bf16[2,2,256,112]{2,3,1,0:T(8,128)(2,1)S(1)}, bf16[2,2,256,112]{2,3,1,0:T(8,128)(2,1)}, u32[]{:S(2)}) copy-start(bf16[2,2,256,112]{2,3,1,0:T(8,128)(2,1)} %get-tuple-element.393) | copy-start | bytes 688132 | tf_op jit(solution)/shard_map/while
  77.8 3.3 %copy-start.10 = (bf16[2,2,256,112]{2,3,1,0:T(8,128)(2,1)}, bf16[2,2,256,112]{2,3,1,0:T(8,128)(2,1)S(1)}, u32[]{:S(2)}) copy-start(bf16[2,2,256,112]{2,3,1,0:T(8,128)(2,1)S(1)} %fusion.139) | copy-start | bytes 688132 | tf_op jit(solution)/shard_map/while
  84.4 2.6 %copy-start.1 = (f32[2,2,256,273]{2,0,3,1:T(2,128)S(1)}, f32[2,2,256,273]{2,0,3,1:T(2,128)}, u32[]{:S(2)}) copy-start(f32[2,2,256,273]{2,0,3,1:T(2,128)} %get-tuple-element.411) | copy-start | bytes 3354628 | tf_op jit(solution)/shard_map/while
  84.4 2.6 %copy-start.2 = (f32[2,2,256,273]{2,0,3,1:T(2,128)S(1)}, f32[2,2,256,273]{2,0,3,1:T(2,128)}, u32[]{:S(2)}) copy-start(f32[2,2,256,273]{2,0,3,1:T(2,128)} %get-tuple-element.415) | copy-start | bytes 3354628 | tf_op jit(solution)/shard_map/while
  86.9 2.5 %copy-start.9 = (bf16[2,2,256,112]{2,3,1,0:T(8,128)(2,1)S(1)}, bf16[2,2,256,112]{2,3,1,0:T(8,128)(2,1)}, u32[]{:S(2)}) copy-start(bf16[2,2,256,112]{2,3,1,0:T(8,128)(2,1)} %get-tuple-element.393) | copy-start | bytes 688132 | tf_op jit(solution)/shard_map/while
  89.9 3.3 %copy-start.10 = (bf16[2,2,256,112]{2,3,1,0:T(8,128)(2,1)}, bf16[2,2,256,112]{2,3,1,0:T(8,128)(2,1)S(1)}, u32[]{:S(2)}) copy-start(bf16[2,2,256,112]{2,3,1,0:T(8,128)(2,1)S(1)} %fusion.139) | copy-start | bytes 688132 | tf_op jit(solution)/shard_map/while
  93.8 3.2 %copy-start.17 = (f32[2,2,256]{2,1,0:T(2,128)}, f32[2,2,256]{2,1,0:T(2,128)S(1)}, u32[]{:S(2)}) copy-start(f32[2,2,256]{2,1,0:T(2,128)S(1)} %get-tuple-element.189) | copy-start | bytes 12292
  99.1 82.8 %all-gather.5.cloned.1.call-start = ((), (), s32[]{:S(2)}) async-start(), calls=%async_computation.4 | async-start | bytes 2064384 | tf_op jit(solution)/shard_map/all_gather | solution.py:224
  (4 other events, 6.5 us)
Sparse Core Ops, SparseCore 0:
  10.6 54.6 all-gather.2
  99.2 41.6 reduce-scatter.1
  142.7 39.1 all-gather.4
where the time goes:
time: 209 us; the launch traced here: 208 us
  waiting for transfers between devices  93 us (44%)
  local copies, waits for them, and re-layouts  29 us (14%)
  matrix products  28.1 us (13%)
  blocking collectives  16.1 us (8%)
  between operations  15.6 us (7%)
  other arithmetic  12.8 us (6%)
  starting transfers between devices  10.7 us (5%)
  loops' own time  2.99 us (1%)
    reduce_scatter x1, waiting for transfers between devices, on_device(): lax.psum_scatter(partial_value.astype(jnp.bfloat16), 'mp', scatter_dimens...  40 us
    all_gather x1, waiting for transfers between devices, on_device(): group_rows = lax.all_gather(final_rows, 'mp', axis=1, tiled=True)  39.3 us
    pmax x1, blocking collectives, on_device(): lax.pmax(partial_best, 'mp')  16.1 us
    all_to_all x1, waiting for transfers between devices, on_device(): lax.all_to_all(jnp.concatenate([kept_pages, projected_pages, lowered_page...  8.43 us
    all_to_all x1, starting transfers between devices, on_device(): lax.all_to_all(jnp.concatenate([kept_pages, projected_pages, lowered_page...  7.62 us
    reshape x3, local copies, waits for them, and re-layouts, regroup(): values.reshape(values.shape[0], blocks, block_len, values.shape[-1])  4.69 us
    ppermute x1, waiting for transfers between devices, from_behind(): return lax.ppermute(value, axis, pairs)  4.52 us
  transfers between devices with their start and end apart: 5, of which 4 were waited for; matrix products, arithmetic and copies ran while one was open for 29% of the time, Pallas kernels for 0%

commit v1 on v0

--- a/solution.py
+++ b/solution.py
@@ -2,6 +2,7 @@
 import jax.numpy as jnp
 from jax import lax
 from jax.sharding import PartitionSpec as P
+from jax.lax import all_to_all, axis_size
 
 FEAT = 16
 HD = 112
@@ -221,7 +222,8 @@
         partial_value.astype(jnp.bfloat16), "mp", scatter_dimension=1, tiled=True
     )
     final_rows = (residual.astype(jnp.float32) + summed.astype(jnp.float32)).astype(jnp.bfloat16)
-    group_rows = lax.all_gather(final_rows, "mp", axis=1, tiled=True)
+    latest = all_to_all(jnp.stack([final_rows for _ in range(axis_size("mp"))], axis=0), "mp", 0, 0)
+    group_rows = jnp.concatenate(latest, 1)
     partial_best = best_of(group_rows, group_vocab)
     max_logits = lax.dynamic_slice_in_dim(
         lax.pmax(partial_best, "mp"), own_shard * (rows_here // shards), rows_here // shards

time: 209 us -> 216 us (1.033)
  starting transfers between devices: 10.7 us -> 15 us
  waiting for transfers between devices: 93 us -> 96 us
    all_to_all x0 -> x1, waiting for transfers between devices: none -> 42.3 us  [on_device(): all_to_all(jnp.stack([final_rows for _ in range(axis_size('mp'))], axis=0...]
    all_gather x1 -> x0, waiting for transfers between devices: 39.3 us -> none  [on_device(): group_rows = lax.all_gather(final_rows, 'mp', axis=1, tiled=True)]
    all_to_all x0 -> x1, starting transfers between devices: none -> 4.33 us  [on_device(): all_to_all(jnp.stack([final_rows for _ in range(axis_size('mp'))], axis=0...]
  transfers between devices with their start and end apart: 5 -> 5, of which waited for: 4 -> 4; matrix products, arithmetic and copies ran while one was open for 29% -> 28% of each run, Pallas kernels for 0% -> 0%
where the time goes in v1:
time: 216 us; the launch traced here: 215 us
  waiting for transfers between devices  96 us (44%)
  local copies, waits for them, and re-layouts  30.4 us (14%)
  matrix products  28.1 us (13%)
  between operations  15.9 us (7%)
  starting transfers between devices  15 us (7%)
  blocking collectives  14.7 us (7%)
  other arithmetic  12.1 us (6%)
  loops' own time  2.99 us (1%)
    all_to_all x1, waiting for transfers between devices, on_device(): all_to_all(jnp.stack([final_rows for _ in range(axis_size('mp'))], axis=0...  42.3 us
    reduce_scatter x1, waiting for transfers between devices, on_device(): lax.psum_scatter(partial_value.astype(jnp.bfloat16), 'mp', scatter_dimens...  40 us
    pmax x1, blocking collectives, on_device(): lax.pmax(partial_best, 'mp')  14.7 us
    all_to_all x1, waiting for transfers between devices, on_device(): lax.all_to_all(jnp.concatenate([kept_pages, projected_pages, lowered_page...  8.43 us
    all_to_all x1, starting transfers between devices, on_device(): lax.all_to_all(jnp.concatenate([kept_pages, projected_pages, lowered_page...  7.62 us
    reshape x3, local copies, waits for them, and re-layouts, regroup(): values.reshape(values.shape[0], blocks, block_len, values.shape[-1])  4.69 us
    ppermute x1, waiting for transfers between devices, from_behind(): return lax.ppermute(value, axis, pairs)  4.52 us
    all_to_all x1, starting transfers between devices, on_device(): all_to_all(jnp.stack([final_rows for _ in range(axis_size('mp'))], axis=0...  4.33 us
  transfers between devices with their start and end apart: 5, of which 4 were waited for; matrix products, arithmetic and copies ran while one was open for 28% of the time, Pallas kernels for 0%

profile of v1, /device:TPU:2, one launch (start us, length us, event | category | flops | bytes accessed | tf_op | source)
XLA Modules:
  0.0 215.3 jit_solution(14951046541035961520)
XLA Ops:
  11.3 1.9 gather_fusion
  13.2 2.0 fusion.49
  16.6 2.3 %fusion.59 = bf16[32,2,8,128]{3,2,1,0:T(8,128)(2,1)S(1)} fusion(bf16[32,2,8,1792]{3,2,1,0:T(8,128)(2,1)} %bitcast.228, f32[1792]{0:T(1024)S(1)} %copy-done.16, f32[32,2,8]{2,1,0:T(2,128)S(1)} %copy.94, bf16[1792,128]{1,0:T(8,128)(2,1)S(1)} %copy-done.15), kind=kOutput, calls=%fused_computation.84 | convolution fusion | flops 238616576 | bytes 2434048 | tf_op jit(solution)/shard_map/abrd,dc->abrc/dot_general | solution.py:118
  21.3 7.6 %all-to-all-start = ((bf16[32,2,8,640]{3,2,1,0:T(8,128)(2,1)}), bf16[32,2,8,640]{3,2,1,0:T(8,128)(2,1)S(1)}, u32[]{:S(2)}, u32[]{:S(2)}) async-start(bf16[32,2,8,640]{3,2,1,0:T(8,128)(2,1)} %pad_maximum_fusion.2), calls=%async_computation | async-start | bytes 1310720 | tf_op jit(solution)/shard_map/all_to_all | solution.py:123
  31.7 8.4 %all-to-all-done = bf16[32,2,8,640]{3,2,1,0:T(8,128)(2,1)S(1)} async-done(((bf16[32,2,8,640]{3,2,1,0:T(8,128)(2,1)}), bf16[32,2,8,640]{3,2,1,0:T(8,128)(2,1)S(1)}, u32[]{:S(2)}, u32[]{:S(2)}) %all-to-all-start) | async-done | bytes 655392 | tf_op jit(solution)/shard_map/all_to_all | solution.py:123
  40.3 1.4 gather_fusion.1
  44.1 1.3 gather_fusion.2
  45.7 2.2 %pad_maximum_fusion.1 = (f32[2,512,273]{1,2,0:T(8,128)}, f32[2,512,273]{1,2,0:T(8,128)S(1)}) fusion(f32[2,512,256]{1,2,0:T(8,128)S(1)} %bitcast.230, f32[2,512,16]{1,2,0:T(8,128)} %get-tuple-element.273, f32[273]{0:T(512)S(1)} %pad.3.clone, f32[2,512,256]{1,2,0:T(8,128)S(1)} %bitcast.231, f32[2,512,16]{1,2,0:T(8,128)} %get-tuple-element.274), kind=kLoop, calls=%fused_computation.86 | loop fusion | flops 1118208 | bytes 4465732 | tf_op jit(solution)/shard_map/concatenate | solution.py:33
  47.9 1.7 reshape.264
  49.6 2.3 %convolution_convert_fusion = bf16[2,273,112]{2,1,0:T(8,128)(2,1)} fusion(f32[2,512,273]{1,2,0:T(8,128)S(1)} %get-tuple-element.280, f32[512]{0:T(512)S(1)} %get-tuple-element.265, bf16[2,512,144]{1,2,0:T(8,128)(2,1)} %bitcast.233), kind=kOutput, calls=%fused_computation.83 | convolution fusion | flops 376058592 | bytes 1471936 | tf_op jit(solution)/shard_map/hcp,hce->hpe/dot_general | solution.py:159
  51.9 1.8 reshape.259
  53.7 3.0 %reshape.268 = f32[2,2,256,273]{2,1,3,0:T(2,128)} reshape(f32[2,512,273]{1,2,0:T(8,128)} %get-tuple-element.279) | data formatting | bytes 2236416 | tf_op jit(solution)/shard_map/reshape | solution.py:181
  57.4 2.1 concatenate.15
  59.5 2.9 %collective-permute-start = (bf16[61699]{0:T(1024)(128)(2,1)S(1)}, bf16[61699]{0:T(1024)(128)(2,1)S(1)}, u32[]{:S(2)}, u32[]{:S(2)}) collective-permute-start(bf16[61699]{0:T(1024)(128)(2,1)S(1)} %concatenate.15), channel_id=1, source_target_pairs={{0,8},{8,16},{16,24},{24,32},{32,40},{40,48},{48,56},{56,64},{64,7... | collective-permute-start | bytes 370202 | tf_op jit(solution)/shard_map/ppermute | solution.py:17
  63.3 4.5 %collective-permute-done = bf16[61699]{0:T(1024)(128)(2,1)S(1)} collective-permute-done((bf16[61699]{0:T(1024)(128)(2,1)S(1)}, bf16[61699]{0:T(1024)(128)(2,1)S(1)}, u32[]{:S(2)}, u32[]{:S(2)}) %collective-permute-start) | collective-permute-done | bytes 123430 | tf_op jit(solution)/shard_map/ppermute | solution.py:17
  69.6 24.2 %while.21 = (s32[]{:T(128)}, f32[2,273,112]{2,1,0:T(8,128)S(1)}, f32[2,273]{0,1:T(8,128)S(1)}, s32[]{:T(128)}, bf16[2,2,256,112]{2,3,1,0:T(8,128)(2,1)}, /*index...) while((s32[]{:T(128)}, f32[2,273,112]{2,1,0:T(8,128)S(1)}, ...), condition=%wide.region_10.11_spmd, body=%wide.region_4.10_spmd.sunk | while | flops 1377437056 | bytes 23302216 | solution.py:196
  95.1 1.9 fusion.81
  97.1 2.0 add_convert_fusion
  100.8 40.0 %reduce-scatter.2.cloned.1.call-done = bf16[512,224]{0,1:T(8,128)(2,1)} async-done(((bf16[512,1792]{0,1:T(8,128)(2,1)}), bf16[512,224]{0,1:T(8,128)(2,1)}) %reduce-scatter.2.cloned.1.call-update) | async-done | bytes 229392 | tf_op jit(solution)/shard_map/reduce_scatter | solution.py:221
  141.9 1.4 stack.2
  143.3 4.3 %all-to-all-start.1 = ((bf16[8,512,224]{1,2,0:T(8,128)(2,1)}), bf16[8,512,224]{1,2,0:T(8,128)(2,1)}, u32[]{:S(2)}, u32[]{:S(2)}) async-start(bf16[8,512,224]{1,2,0:T(8,128)(2,1)} %stack.2), calls=%async_computation.2 | async-start | bytes 3670016 | tf_op jit(solution)/shard_map/all_to_all | solution.py:225
  147.6 42.3 %all-to-all-done.1 = bf16[8,512,224]{1,2,0:T(8,128)(2,1)} async-done(((bf16[8,512,224]{1,2,0:T(8,128)(2,1)}), bf16[8,512,224]{1,2,0:T(8,128)(2,1)}, u32[]{:S(2)}, u32[]{:S(2)}) %all-to-all-start.1) | async-done | bytes 1835040 | tf_op jit(solution)/shard_map/all_to_all | solution.py:225
  190.0 3.2 %convolution_reduce_fusion = f32[512]{0:T(512)S(1)} fusion(bf16[512,1792]{1,0:T(8,128)(2,1)} %all-gather.2.cloned.1.call-done, bf16[512,1792]{0,1:T(8,128)(2,1)} %bitcast.48), kind=kOutput, calls=%fused_computation.82 | convolution fusion | flops 939785728 | bytes 3672064 | tf_op jit(solution)/shard_map/rd,vd->rv/dot_general | solution.py:80
  193.1 14.7 %pmax.7 = f32[512]{0:T(512)S(1)} all-reduce(f32[512]{0:T(512)S(1)} %convolution_reduce_fusion), channel_id=1, replica_groups=mesh['group'=32,'mp'=8] {'mp'}, use_global_device_ids=true, to_apply=%region_15.16 | all-reduce | flops 512 | bytes 4096 | tf_op jit(solution)/shard_map/pmax | solution.py:229
  (164 shorter events, 41.2 us)
Async XLA Ops:
  7.2 4.1 %copy-start = (bf16[512,1792]{1,0:T(8,128)(2,1)S(1)}, bf16[512,1792]{1,0:T(8,128)(2,1)}, u32[]{:S(2)}) copy-start(bf16[512,1792]{1,0:T(8,128)(2,1)} %param.13) | copy-start | bytes 5505028
  7.2 87.9 %all-gather.2.cloned.1.call-start = ((), (), s32[]{:S(2)}) async-start(), calls=%async_computation.3 | async-start | bytes 1892352 | tf_op jit(solution)/shard_map/all_gather | solution.py:147
  13.2 3.3 %copy-start.15 = (bf16[1792,128]{1,0:T(8,128)(2,1)S(1)}, bf16[1792,128]{1,0:T(8,128)(2,1)}, u32[]{:S(2)}) copy-start(bf16[1792,128]{1,0:T(8,128)(2,1)} %param.17) | copy-start | bytes 1376260
  13.2 3.3 %copy-start.16 = (f32[1792]{0:T(1024)S(1)}, f32[1792]{0:T(1024)}, u32[]{:S(2)}) copy-start(f32[1792]{0:T(1024)} %param.14) | copy-start | bytes 21508
  16.5 2.4 %copy-start.3 = (bf16[64,8,1792]{2,1,0:T(8,128)(2,1)S(1)}, bf16[64,8,1792]{2,1,0:T(8,128)(2,1)}, u32[]{:S(2)}) copy-start(bf16[64,8,1792]{2,1,0:T(8,128)(2,1)} %gather_fusion) | copy-start | bytes 5505028
  16.6 2.4 %copy-start.14 = (bf16[1792,288]{0,1:T(8,128)(2,1)S(1)}, bf16[1792,288]{0,1:T(8,128)(2,1)}, u32[]{:S(2)}) copy-start(bf16[1792,288]{0,1:T(8,128)(2,1)} %param.15) | copy-start | bytes 3096580
  20.1 8.9 %copy-start.11 = (s32[512]{0:T(512)S(1)}, s32[512]{0:T(512)}, u32[]{:S(2)}) copy-start(s32[512]{0:T(512)} %param.20) | copy-start | bytes 6148
  20.1 11.2 %copy-start.12 = (s32[128]{0:T(128)S(1)}, s32[128]{0:T(128)}, u32[]{:S(2)}) copy-start(s32[128]{0:T(128)} %param.21) | copy-start | bytes 1540
  20.1 11.4 %copy-start.13 = (s32[64]{0:T(128)S(1)}, s32[64]{0:T(128)}, u32[]{:S(2)}) copy-start(s32[64]{0:T(128)} %param.22) | copy-start | bytes 772
  21.3 18.8 %all-to-all-start = ((bf16[32,2,8,640]{3,2,1,0:T(8,128)(2,1)}), bf16[32,2,8,640]{3,2,1,0:T(8,128)(2,1)S(1)}, u32[]{:S(2)}, u32[]{:S(2)}) async-start(bf16[32,2,8,640]{3,2,1,0:T(8,128)(2,1)} %pad_maximum_fusion.2), calls=%async_computation | async-start | bytes 1310720 | tf_op jit(solution)/shard_map/all_to_all | solution.py:123
  28.9 112.0 %reduce-scatter.2.cloned.1.call-start = ((), (), s32[]{:S(2)}) async-start(), calls=%async_computation.4 | async-start | bytes 2064384 | tf_op jit(solution)/shard_map/reduce_scatter | solution.py:221
  40.1 4.0 %copy-start.4 = (bf16[32,2,8,640]{3,2,1,0:T(8,128)(2,1)}, bf16[32,2,8,640]{3,2,1,0:T(8,128)(2,1)S(1)}, u32[]{:S(2)}) copy-start(bf16[32,2,8,640]{3,2,1,0:T(8,128)(2,1)S(1)} %all-to-all-done) | copy-start | bytes 1966084
  43.3 2.4 %copy-start.5 = (bf16[512,2,144]{0,2,1:T(8,128)(2,1)}, bf16[512,2,144]{0,2,1:T(8,128)(2,1)S(1)}, u32[]{:S(2)}) copy-start(bf16[512,2,144]{0,2,1:T(8,128)(2,1)S(1)} %copy.95) | copy-start | bytes 884740
  59.5 8.3 %collective-permute-start = (bf16[61699]{0:T(1024)(128)(2,1)S(1)}, bf16[61699]{0:T(1024)(128)(2,1)S(1)}, u32[]{:S(2)}, u32[]{:S(2)}) collective-permute-start(bf16[61699]{0:T(1024)(128)(2,1)S(1)} %concatenate.15), channel_id=1, source_target_pairs={{0,8},{8,16},{16,24},{24,32},{32,40},{40,48},{48,56},{56,64},{64,7... | collective-permute-start | bytes 370202 | tf_op jit(solution)/shard_map/ppermute | solution.py:17
  72.3 2.6 %copy-start.1 = (f32[2,2,256,273]{2,0,3,1:T(2,128)S(1)}, f32[2,2,256,273]{2,0,3,1:T(2,128)}, u32[]{:S(2)}) copy-start(f32[2,2,256,273]{2,0,3,1:T(2,128)} %get-tuple-element.411) | copy-start | bytes 3354628 | tf_op jit(solution)/shard_map/while
  72.3 2.6 %copy-start.2 = (f32[2,2,256,273]{2,0,3,1:T(2,128)S(1)}, f32[2,2,256,273]{2,0,3,1:T(2,128)}, u32[]{:S(2)}) copy-start(f32[2,2,256,273]{2,0,3,1:T(2,128)} %get-tuple-element.415) | copy-start | bytes 3354628 | tf_op jit(solution)/shard_map/while
  74.8 2.5 %copy-start.9 = (bf16[2,2,256,112]{2,3,1,0:T(8,128)(2,1)S(1)}, bf16[2,2,256,112]{2,3,1,0:T(8,128)(2,1)}, u32[]{:S(2)}) copy-start(bf16[2,2,256,112]{2,3,1,0:T(8,128)(2,1)} %get-tuple-element.393) | copy-start | bytes 688132 | tf_op jit(solution)/shard_map/while
  77.8 3.3 %copy-start.10 = (bf16[2,2,256,112]{2,3,1,0:T(8,128)(2,1)}, bf16[2,2,256,112]{2,3,1,0:T(8,128)(2,1)S(1)}, u32[]{:S(2)}) copy-start(bf16[2,2,256,112]{2,3,1,0:T(8,128)(2,1)S(1)} %fusion.139) | copy-start | bytes 688132 | tf_op jit(solution)/shard_map/while
  84.4 2.6 %copy-start.1 = (f32[2,2,256,273]{2,0,3,1:T(2,128)S(1)}, f32[2,2,256,273]{2,0,3,1:T(2,128)}, u32[]{:S(2)}) copy-start(f32[2,2,256,273]{2,0,3,1:T(2,128)} %get-tuple-element.411) | copy-start | bytes 3354628 | tf_op jit(solution)/shard_map/while
  84.4 2.6 %copy-start.2 = (f32[2,2,256,273]{2,0,3,1:T(2,128)S(1)}, f32[2,2,256,273]{2,0,3,1:T(2,128)}, u32[]{:S(2)}) copy-start(f32[2,2,256,273]{2,0,3,1:T(2,128)} %get-tuple-element.415) | copy-start | bytes 3354628 | tf_op jit(solution)/shard_map/while
  86.9 2.5 %copy-start.9 = (bf16[2,2,256,112]{2,3,1,0:T(8,128)(2,1)S(1)}, bf16[2,2,256,112]{2,3,1,0:T(8,128)(2,1)}, u32[]{:S(2)}) copy-start(bf16[2,2,256,112]{2,3,1,0:T(8,128)(2,1)} %get-tuple-element.393) | copy-start | bytes 688132 | tf_op jit(solution)/shard_map/while
  89.9 3.3 %copy-start.10 = (bf16[2,2,256,112]{2,3,1,0:T(8,128)(2,1)}, bf16[2,2,256,112]{2,3,1,0:T(8,128)(2,1)S(1)}, u32[]{:S(2)}) copy-start(bf16[2,2,256,112]{2,3,1,0:T(8,128)(2,1)S(1)} %fusion.139) | copy-start | bytes 688132 | tf_op jit(solution)/shard_map/while
  93.8 3.2 %copy-start.17 = (f32[2,2,256]{2,1,0:T(2,128)}, f32[2,2,256]{2,1,0:T(2,128)S(1)}, u32[]{:S(2)}) copy-start(f32[2,2,256]{2,1,0:T(2,128)S(1)} %get-tuple-element.189) | copy-start | bytes 12292
  143.3 46.7 %all-to-all-start.1 = ((bf16[8,512,224]{1,2,0:T(8,128)(2,1)}), bf16[8,512,224]{1,2,0:T(8,128)(2,1)}, u32[]{:S(2)}, u32[]{:S(2)}) async-start(bf16[8,512,224]{1,2,0:T(8,128)(2,1)} %stack.2), calls=%async_computation.2 | async-start | bytes 3670016 | tf_op jit(solution)/shard_map/all_to_all | solution.py:225
  (4 other events, 6.5 us)
Sparse Core Ops, SparseCore 0:
  10.6 54.6 all-gather.1
  99.2 41.6 reduce-scatter.1
